TPU v7x, 128 devices: a whole 4x4x4 slice. The times are simulated.
128 devices in a mesh: users: 32 (over z, x, core), items: 4 (over y).
Axes of the slice: x: 4, y: 4, z: 4, core: 2. Of those that a mesh axis runs over, the one named last changes fastest.
Arguments:
- user_factors: bfloat16 [65536, 256], P('users'), may hold values from -1.5 to 1.5
- item_factors: bfloat16 [4, 4096, 256], P('items', 'users'), may hold values from -1.5 to 1.5
- confidence: bfloat16 [32, 4, 256, 128, 128], P('users', 'items'), may hold values from 0.099609375 to 10
- tile_counts: int32 [32, 4, 256], P('users', 'items'), may hold values from 1 to 4095
- tile_user: int32 [32, 4, 256], P('users', 'items'), may hold values from 0 to 15
- tile_item: int32 [32, 4, 256], P('users', 'items'), may hold values from 0 to 31
- block_slot: int32 [4, 32], P('items'), may hold values from 0 to 31, each once within a row
- live_tiles: int32 [32, 4], P('users', 'items'), may hold values from 64 to 256, as said below
Outputs:
- user_grad: float32 [65536, 256], P('users')
- item_grad: float32 [4, 4096, 256], P('items', 'users')
Inputs may be any that keep to these rules, and one draw needn't show every extreme that they name: Tile slots at positions from live_tiles on are ignored; some user shard and group uses all 256 slots.
All inputs are finite; a program needn't handle non-finite values.
Results may differ from a plain program's by a relative error of at most 0.0012.
Values may be sent and summed in bfloat16 or wider, within the bound.
No kernel may reach another device: no remote copies, remote signals or barrier semaphores. Data moves between devices by JAX's collectives and lax.ppermute only.
A program may use at most 128 MiB of HBM per device.

v0:
```python
import math
import jax
import jax.numpy as jnp
from jax import lax
from jax.sharding import PartitionSpec as P

grad_scale = 0.005
gram_weight = 0.5


def gramian(factor_rows):
    return lax.dot_general(
        factor_rows, factor_rows, (((0,), (0,)), ((), ())), preferred_element_type=jnp.float32
    )


def local(
    user_factors,
    item_factors,
    confidence,
    tile_counts,
    tile_user,
    tile_item,
    block_slot,
    live_tiles,
):
    row_count, rank_size = user_factors.shape
    tile_edge = confidence.shape[3]
    user_block_count = row_count // tile_edge
    user_blocks = user_factors.reshape(user_block_count, tile_edge, rank_size)
    gathered = lax.all_gather(item_factors, "users", axis=1, tiled=True)[0]
    panel_count = gathered.shape[0] // tile_edge
    item_blocks = gathered.reshape(panel_count, tile_edge, rank_size)
    confidence_tiles = confidence[0, 0]
    user_list = tile_user[0, 0]
    slot_list = block_slot[0][tile_item[0, 0]]
    tile_scale = jnp.log1p(tile_counts[0, 0].astype(jnp.float32))
    live_count = live_tiles[0, 0]
    tile_total = confidence_tiles.shape[0]
    step_tiles = math.gcd(tile_total, 32)
    user_ids = jnp.arange(user_block_count, dtype=jnp.int32)
    panel_ids = jnp.arange(panel_count, dtype=jnp.int32)

    def visit_block(block_number, state_pair):
        user_acc, item_acc = state_pair
        first_tile = block_number * step_tiles
        conf_block = lax.dynamic_slice_in_dim(confidence_tiles, first_tile, step_tiles, 0)
        user_pick = lax.dynamic_slice_in_dim(user_list, first_tile, step_tiles, 0)
        slot_pick = lax.dynamic_slice_in_dim(slot_list, first_tile, step_tiles, 0)
        scale_pick = lax.dynamic_slice_in_dim(tile_scale, first_tile, step_tiles, 0)
        live_mask = (first_tile + jnp.arange(step_tiles, dtype=jnp.int32) < live_count).astype(
            jnp.float32
        )
        user_hot = user_pick[:, None] == user_ids[None, :]
        panel_hot = slot_pick[:, None] == panel_ids[None, :]
        user_tiles = jnp.einsum(
            "tu,uak->tak",
            user_hot.astype(jnp.bfloat16),
            user_blocks,
            preferred_element_type=jnp.float32,
        ).astype(jnp.bfloat16)
        item_tiles = jnp.einsum(
            "tp,pak->tak",
            panel_hot.astype(jnp.bfloat16),
            item_blocks,
            preferred_element_type=jnp.float32,
        ).astype(jnp.bfloat16)
        scores = jnp.einsum(
            "tak,tbk->tab", user_tiles, item_tiles, preferred_element_type=jnp.float32
        )
        factor = (scale_pick * live_mask)[:, None, None]
        weighted = (conf_block.astype(jnp.float32) * factor * (scores - 1.0)).astype(jnp.bfloat16)
        user_terms = jnp.einsum(
            "tab,tbk->tak", weighted, item_tiles, preferred_element_type=jnp.float32
        )
        item_terms = jnp.einsum(
            "tab,tak->tbk", weighted, user_tiles, preferred_element_type=jnp.float32
        )
        user_acc = user_acc + jnp.einsum(
            "tu,tak->uak", user_hot.astype(jnp.float32), user_terms, precision=lax.Precision.HIGHEST
        )
        item_acc = item_acc + jnp.einsum(
            "tp,tak->pak",
            panel_hot.astype(jnp.float32),
            item_terms,
            precision=lax.Precision.HIGHEST,
        )
        return (user_acc, item_acc)

    start_pair = (
        jnp.zeros((user_block_count, tile_edge, rank_size), jnp.float32),
        jnp.zeros((panel_count, tile_edge, rank_size), jnp.float32),
    )
    user_acc, item_acc = lax.fori_loop(0, tile_total // step_tiles, visit_block, start_pair)
    user_part = grad_scale * user_acc.reshape(row_count, rank_size)
    item_part = grad_scale * item_acc.reshape(panel_count * tile_edge, rank_size)
    own_panels = item_factors[0]
    user_wide = user_factors.astype(jnp.float32)
    own_wide = own_panels.astype(jnp.float32)
    item_gram = lax.psum(gramian(own_panels), ("users", "items"))
    user_total = lax.psum(user_part, "items")
    user_grad = user_total + grad_scale * gram_weight * jnp.dot(
        user_wide, item_gram, precision=lax.Precision.HIGHEST
    )
    item_total = lax.psum_scatter(item_part, "users", scatter_dimension=0, tiled=True)
    user_gram = lax.psum(gramian(user_factors).astype(jnp.bfloat16), "users").astype(jnp.float32)
    item_grad = item_total + grad_scale * gram_weight * jnp.dot(
        own_wide, user_gram, precision=lax.Precision.HIGHEST
    )
    return (user_grad, item_grad[None])


def solution(mesh):
    in_specs = (
        P("users", None),
        P("items", "users", None),
        P("users", "items", None, None, None),
        P("users", "items", None),
        P("users", "items", None),
        P("users", "items", None),
        P("items", None),
        P("users", "items"),
    )
    out_specs = (P("users", None), P("items", "users", None))
    return jax.shard_map(local, mesh=mesh, in_specs=in_specs, out_specs=out_specs, check_vma=False)
```

profile of v0, /device:TPU:0, one launch (start us, length us, event | category | flops | bytes accessed | tf_op | source)
XLA Modules:
  0.0 557.9 jit_solution(8416958373465999257)
XLA Ops:
  21.6 15.7 %select_select_fusion = s32[256]{0:T(256)S(1)} fusion(pred[256]{0:T(512)(128)(4,1)S(1)} %get-tuple-element.366, pred[256]{0:T(512)(128)(4,1)S(1)} %get-tuple-element.365, pred[256]{0:T(512)(128)(4,1)S(1)} %get-tuple-element.364, pred[256]{0:T(512)(128)(4,1)S(1)} %get-tuple-element.363, pred[256]{0:T(512)(128)(4,1)S(1)} %get-tuple-element.362, ...), kind=kLoop, calls=%fused_computation.84 | loop fusion | flops 6400 | bytes 8548 | tf_op jit(solution)/shard_map/gather | solution.py:36
  37.3 20.1 %all-gather.2.cloned.1.call-done = bf16[1,4096,256]{2,1,0:T(8,128)(2,1)} async-done(((bf16[1,128,256]{2,1,0:T(8,128)(2,1)}), bf16[1,4096,256]{2,1,0:T(8,128)(2,1)}) %all-gather.2.cloned.1.call-update) | async-done | bytes 2097168 | tf_op jit(solution)/shard_map/all_gather | solution.py:31
  60.2 232.7 %while.18 = (s32[]{:T(128)}, f32[16,128,256]{2,0,1:T(8,128)}, f32[32,128,256]{2,0,1:T(8,128)}, s32[256]{0:T(256)S(1)}, bf16[256,128,128]{2,1,0:T(8,128)(2,1)}, /...) while((s32[]{:T(128)}, f32[16,128,256]{2,0,1:T(8,128)}, ...), condition=%wide.region_1.0_spmd.clone, body=%wide.region_0.0_spmd.clone.sunk | while | flops 1520438400 | bytes 120588176 | solution.py:94
  70.5 7.4 %select_add_fusion.4 = f32[16,128,256]{2,0,1:T(8,128)} fusion(f32[16,128,256]{2,0,1:T(8,128)} %get-tuple-element.497, f32[32,128,256]{2,1,0:T(8,128)} %fusion.84, pred[]{:T(512)S(6)} %compare.128, s32[32]{0:T(128)S(1)} %dynamic_slice.62), kind=kOutput, calls=%fused_computation.7.clone.1 | convolution fusion | flops 202375680 | bytes 8388737 | tf_op jit(solution)/shard_map/while/body/eval_jaxpr/tu,tak->uak/dot_general | solution.py:79
  81.7 5.2 select_add_fusion.5
  99.0 8.1 %select_add_fusion.4 = f32[16,128,256]{2,0,1:T(8,128)} fusion(f32[16,128,256]{2,0,1:T(8,128)} %get-tuple-element.497, f32[32,128,256]{2,1,0:T(8,128)} %fusion.84, pred[]{:T(512)S(6)} %compare.128, s32[32]{0:T(128)S(1)} %dynamic_slice.62), kind=kOutput, calls=%fused_computation.7.clone.1 | convolution fusion | flops 202375680 | bytes 8388737 | tf_op jit(solution)/shard_map/while/body/eval_jaxpr/tu,tak->uak/dot_general | solution.py:79
  110.9 5.2 select_add_fusion.5
  128.1 8.1 %select_add_fusion.4 = f32[16,128,256]{2,0,1:T(8,128)} fusion(f32[16,128,256]{2,0,1:T(8,128)} %get-tuple-element.497, f32[32,128,256]{2,1,0:T(8,128)} %fusion.84, pred[]{:T(512)S(6)} %compare.128, s32[32]{0:T(128)S(1)} %dynamic_slice.62), kind=kOutput, calls=%fused_computation.7.clone.1 | convolution fusion | flops 202375680 | bytes 8388737 | tf_op jit(solution)/shard_map/while/body/eval_jaxpr/tu,tak->uak/dot_general | solution.py:79
  140.0 5.2 select_add_fusion.5
  157.3 8.1 %select_add_fusion.4 = f32[16,128,256]{2,0,1:T(8,128)} fusion(f32[16,128,256]{2,0,1:T(8,128)} %get-tuple-element.497, f32[32,128,256]{2,1,0:T(8,128)} %fusion.84, pred[]{:T(512)S(6)} %compare.128, s32[32]{0:T(128)S(1)} %dynamic_slice.62), kind=kOutput, calls=%fused_computation.7.clone.1 | convolution fusion | flops 202375680 | bytes 8388737 | tf_op jit(solution)/shard_map/while/body/eval_jaxpr/tu,tak->uak/dot_general | solution.py:79
  169.2 5.2 select_add_fusion.5
  186.4 8.1 %select_add_fusion.4 = f32[16,128,256]{2,0,1:T(8,128)} fusion(f32[16,128,256]{2,0,1:T(8,128)} %get-tuple-element.497, f32[32,128,256]{2,1,0:T(8,128)} %fusion.84, pred[]{:T(512)S(6)} %compare.128, s32[32]{0:T(128)S(1)} %dynamic_slice.62), kind=kOutput, calls=%fused_computation.7.clone.1 | convolution fusion | flops 202375680 | bytes 8388737 | tf_op jit(solution)/shard_map/while/body/eval_jaxpr/tu,tak->uak/dot_general | solution.py:79
  198.3 5.2 select_add_fusion.5
  215.6 8.1 %select_add_fusion.4 = f32[16,128,256]{2,0,1:T(8,128)} fusion(f32[16,128,256]{2,0,1:T(8,128)} %get-tuple-element.497, f32[32,128,256]{2,1,0:T(8,128)} %fusion.84, pred[]{:T(512)S(6)} %compare.128, s32[32]{0:T(128)S(1)} %dynamic_slice.62), kind=kOutput, calls=%fused_computation.7.clone.1 | convolution fusion | flops 202375680 | bytes 8388737 | tf_op jit(solution)/shard_map/while/body/eval_jaxpr/tu,tak->uak/dot_general | solution.py:79
  227.5 5.2 select_add_fusion.5
  244.7 8.1 %select_add_fusion.4 = f32[16,128,256]{2,0,1:T(8,128)} fusion(f32[16,128,256]{2,0,1:T(8,128)} %get-tuple-element.497, f32[32,128,256]{2,1,0:T(8,128)} %fusion.84, pred[]{:T(512)S(6)} %compare.128, s32[32]{0:T(128)S(1)} %dynamic_slice.62), kind=kOutput, calls=%fused_computation.7.clone.1 | convolution fusion | flops 202375680 | bytes 8388737 | tf_op jit(solution)/shard_map/while/body/eval_jaxpr/tu,tak->uak/dot_general | solution.py:79
  256.6 5.2 select_add_fusion.5
  273.9 8.1 %select_add_fusion.4 = f32[16,128,256]{2,0,1:T(8,128)} fusion(f32[16,128,256]{2,0,1:T(8,128)} %get-tuple-element.497, f32[32,128,256]{2,1,0:T(8,128)} %fusion.84, pred[]{:T(512)S(6)} %compare.128, s32[32]{0:T(128)S(1)} %dynamic_slice.62), kind=kOutput, calls=%fused_computation.7.clone.1 | convolution fusion | flops 202375680 | bytes 8388737 | tf_op jit(solution)/shard_map/while/body/eval_jaxpr/tu,tak->uak/dot_general | solution.py:79
  285.8 5.2 select_add_fusion.5
  308.3 5.9 %copy.23 = f32[32,128,256]{1,0,2:T(8,128)} copy(f32[32,128,256]{2,0,1:T(8,128)} %broadcast_multiply_fusion) | data formatting | bytes 8388608 | tf_op jit(solution)/shard_map/mul | solution.py:96
  314.3 7.9 %copy.50 = f32[32,8,32,128]{3,1,2,0:T(8,128)} copy(f32[32,8,32,128]{3,2,1,0:T(8,128)} %bitcast.100) | data formatting | bytes 8388608
  322.3 36.4 %all-reduce.4.cloned.1.call-done = f32[2048,256]{0,1:T(8,128)} async-done(((f32[2048,256]{0,1:T(8,128)}), f32[2048,256]{0,1:T(8,128)}) %all-reduce.4.cloned.1.call-update) | async-done | bytes 2097168 | tf_op jit(solution)/shard_map/psum | solution.py:101
  364.0 98.7 %all-reduce.8.cloned.1.call-done = bf16[256,256]{1,0:T(8,128)(2,1)} async-done(((bf16[256,256]{1,0:T(8,128)(2,1)}), bf16[256,256]{1,0:T(8,128)(2,1)}) %all-reduce.8.cloned.1.call-update) | async-done | bytes 131088 | tf_op jit(solution)/shard_map/psum | solution.py:106
  462.7 85.6 %reduce-scatter.2.cloned.1.call-done = f32[128,256]{0,1:T(8,128)} async-done(((f32[4096,256]{0,1:T(8,128)}), f32[128,256]{0,1:T(8,128)}) %reduce-scatter.2.cloned.1.call-update) | async-done | bytes 131088 | tf_op jit(solution)/shard_map/reduce_scatter | solution.py:105
  (198 shorter events, 165.4 us)
Async XLA Ops:
  8.0 9.1 %copy-start.8 = (s32[1,1,256]{2,1,0:T(1,128)S(1)}, s32[1,1,256]{2,1,0:T(1,128)}, u32[]{:S(2)}) copy-start(s32[1,1,256]{2,1,0:T(1,128)} %param.15) | copy-start | bytes 3076
  8.0 49.4 %all-gather.2.cloned.1.call-start = ((), (), s32[]{:S(2)}) async-start(), calls=%async_computation.1 | async-start | bytes 2162688 | tf_op jit(solution)/shard_map/all_gather | solution.py:31
  8.7 313.5 %all-reduce.6.cloned.1.call-start = ((), (), s32[]{:S(2)}) async-start(), calls=%async_computation.3 | async-start | bytes 524288 | tf_op jit(solution)/shard_map/psum | solution.py:100
  10.6 348.0 %all-reduce.4.cloned.1.call-start = ((), (), s32[]{:S(2)}) async-start(), calls=%async_computation.2 | async-start | bytes 4194304 | tf_op jit(solution)/shard_map/psum | solution.py:101
  70.5 7.4 %copy-start.1 = (bf16[32,128,256]{2,0,1:T(8,128)(2,1)S(1)}, bf16[32,128,256]{2,0,1:T(8,128)(2,1)}, u32[]{:S(2)}) copy-start(bf16[32,128,256]{2,0,1:T(8,128)(2,1)} %copy-done) | copy-start | bytes 6291460 | tf_op jit(solution)/shard_map/while
  81.7 7.1 %copy-start.5 = (bf16[32,128,256]{2,0,1:T(8,128)(2,1)S(1)}, bf16[32,128,256]{2,0,1:T(8,128)(2,1)}, u32[]{:S(2)}) copy-start(bf16[32,128,256]{2,0,1:T(8,128)(2,1)} %copy-done.4) | copy-start | bytes 6291460 | tf_op jit(solution)/shard_map/while
  99.0 8.1 %copy-start.1 = (bf16[32,128,256]{2,0,1:T(8,128)(2,1)S(1)}, bf16[32,128,256]{2,0,1:T(8,128)(2,1)}, u32[]{:S(2)}) copy-start(bf16[32,128,256]{2,0,1:T(8,128)(2,1)} %copy-done) | copy-start | bytes 6291460 | tf_op jit(solution)/shard_map/while
  110.9 7.1 %copy-start.5 = (bf16[32,128,256]{2,0,1:T(8,128)(2,1)S(1)}, bf16[32,128,256]{2,0,1:T(8,128)(2,1)}, u32[]{:S(2)}) copy-start(bf16[32,128,256]{2,0,1:T(8,128)(2,1)} %copy-done.4) | copy-start | bytes 6291460 | tf_op jit(solution)/shard_map/while
  128.1 8.1 %copy-start.1 = (bf16[32,128,256]{2,0,1:T(8,128)(2,1)S(1)}, bf16[32,128,256]{2,0,1:T(8,128)(2,1)}, u32[]{:S(2)}) copy-start(bf16[32,128,256]{2,0,1:T(8,128)(2,1)} %copy-done) | copy-start | bytes 6291460 | tf_op jit(solution)/shard_map/while
  136.2 3.8 copy-start.2
  140.0 7.2 %copy-start.5 = (bf16[32,128,256]{2,0,1:T(8,128)(2,1)S(1)}, bf16[32,128,256]{2,0,1:T(8,128)(2,1)}, u32[]{:S(2)}) copy-start(bf16[32,128,256]{2,0,1:T(8,128)(2,1)} %copy-done.4) | copy-start | bytes 6291460 | tf_op jit(solution)/shard_map/while
  157.3 8.1 %copy-start.1 = (bf16[32,128,256]{2,0,1:T(8,128)(2,1)S(1)}, bf16[32,128,256]{2,0,1:T(8,128)(2,1)}, u32[]{:S(2)}) copy-start(bf16[32,128,256]{2,0,1:T(8,128)(2,1)} %copy-done) | copy-start | bytes 6291460 | tf_op jit(solution)/shard_map/while
  169.2 7.1 %copy-start.5 = (bf16[32,128,256]{2,0,1:T(8,128)(2,1)S(1)}, bf16[32,128,256]{2,0,1:T(8,128)(2,1)}, u32[]{:S(2)}) copy-start(bf16[32,128,256]{2,0,1:T(8,128)(2,1)} %copy-done.4) | copy-start | bytes 6291460 | tf_op jit(solution)/shard_map/while
  186.4 8.1 %copy-start.1 = (bf16[32,128,256]{2,0,1:T(8,128)(2,1)S(1)}, bf16[32,128,256]{2,0,1:T(8,128)(2,1)}, u32[]{:S(2)}) copy-start(bf16[32,128,256]{2,0,1:T(8,128)(2,1)} %copy-done) | copy-start | bytes 6291460 | tf_op jit(solution)/shard_map/while
  198.3 7.2 %copy-start.5 = (bf16[32,128,256]{2,0,1:T(8,128)(2,1)S(1)}, bf16[32,128,256]{2,0,1:T(8,128)(2,1)}, u32[]{:S(2)}) copy-start(bf16[32,128,256]{2,0,1:T(8,128)(2,1)} %copy-done.4) | copy-start | bytes 6291460 | tf_op jit(solution)/shard_map/while
  215.6 8.1 %copy-start.1 = (bf16[32,128,256]{2,0,1:T(8,128)(2,1)S(1)}, bf16[32,128,256]{2,0,1:T(8,128)(2,1)}, u32[]{:S(2)}) copy-start(bf16[32,128,256]{2,0,1:T(8,128)(2,1)} %copy-done) | copy-start | bytes 6291460 | tf_op jit(solution)/shard_map/while
  227.5 7.1 %copy-start.5 = (bf16[32,128,256]{2,0,1:T(8,128)(2,1)S(1)}, bf16[32,128,256]{2,0,1:T(8,128)(2,1)}, u32[]{:S(2)}) copy-start(bf16[32,128,256]{2,0,1:T(8,128)(2,1)} %copy-done.4) | copy-start | bytes 6291460 | tf_op jit(solution)/shard_map/while
  244.7 8.1 %copy-start.1 = (bf16[32,128,256]{2,0,1:T(8,128)(2,1)S(1)}, bf16[32,128,256]{2,0,1:T(8,128)(2,1)}, u32[]{:S(2)}) copy-start(bf16[32,128,256]{2,0,1:T(8,128)(2,1)} %copy-done) | copy-start | bytes 6291460 | tf_op jit(solution)/shard_map/while
  256.6 7.2 %copy-start.5 = (bf16[32,128,256]{2,0,1:T(8,128)(2,1)S(1)}, bf16[32,128,256]{2,0,1:T(8,128)(2,1)}, u32[]{:S(2)}) copy-start(bf16[32,128,256]{2,0,1:T(8,128)(2,1)} %copy-done.4) | copy-start | bytes 6291460 | tf_op jit(solution)/shard_map/while
  273.9 8.1 %copy-start.1 = (bf16[32,128,256]{2,0,1:T(8,128)(2,1)S(1)}, bf16[32,128,256]{2,0,1:T(8,128)(2,1)}, u32[]{:S(2)}) copy-start(bf16[32,128,256]{2,0,1:T(8,128)(2,1)} %copy-done) | copy-start | bytes 6291460 | tf_op jit(solution)/shard_map/while
  285.8 7.1 %copy-start.5 = (bf16[32,128,256]{2,0,1:T(8,128)(2,1)S(1)}, bf16[32,128,256]{2,0,1:T(8,128)(2,1)}, u32[]{:S(2)}) copy-start(bf16[32,128,256]{2,0,1:T(8,128)(2,1)} %copy-done.4) | copy-start | bytes 6291460 | tf_op jit(solution)/shard_map/while
  300.8 161.9 %all-reduce.8.cloned.1.call-start = ((), (), s32[]{:S(2)}) async-start(), calls=%async_computation.5 | async-start | bytes 262144 | tf_op jit(solution)/shard_map/psum | solution.py:106
  303.2 245.1 %reduce-scatter.2.cloned.1.call-start = ((), (), s32[]{:S(2)}) async-start(), calls=%async_computation.4 | async-start | bytes 4325376 | tf_op jit(solution)/shard_map/reduce_scatter | solution.py:105
  362.2 186.1 %copy-start.7 = (bf16[1,128,256]{2,1,0:T(8,128)(2,1)S(1)}, bf16[1,128,256]{2,1,0:T(8,128)(2,1)}, u32[]{:S(2)}) copy-start(bf16[1,128,256]{2,1,0:T(8,128)(2,1)} %param.11) | copy-start | bytes 196612
  (33 other events, 76.2 us)
Sparse Core Ops, SparseCore 0:
  11.1 46.2 all-gather.1
Sparse Core Ops, SparseCore 1:
  14.0 147.1 all-reduce.5
  300.9 57.7 all-reduce.3
  362.3 100.3 all-reduce.7
  466.4 81.9 reduce-scatter.1
where the time goes:
time: 559 us; the launch traced here: 558 us
  waiting for transfers between devices  242 us (43%)
  matrix products  213 us (38%)
  local copies, waits for them, and re-layouts  53.3 us (10%)
  other arithmetic  33.6 us (6%)
  between operations  15.8 us (3%)
    psum x1, waiting for transfers between devices, local(): lax.psum(gramian(user_factors).astype(jnp.bfloat16), 'users')  98.7 us
    reduce_scatter x1, waiting for transfers between devices, local(): lax.psum_scatter(item_part, 'users', scatter_dimension=0, tiled=True)  85.6 us
    dot_general x8, matrix products, visit_block(): jnp.einsum('tu,tak->uak', user_hot.astype(jnp.float32), user_terms, preci...  64 us
    dot_general x8, matrix products, visit_block(): jnp.einsum('tp,tak->pak', panel_hot.astype(jnp.float32), item_terms, prec...  41.6 us
    dot_general x8, matrix products, visit_block(): jnp.einsum('tab,tbk->tak', weighted, item_tiles, preferred_element_type=j...  38.1 us
    psum x1, waiting for transfers between devices, local(): user_total = lax.psum(user_part, 'items')  36.4 us
    dot_general x8, matrix products, visit_block(): jnp.einsum('tab,tak->tbk', weighted, user_tiles, preferred_element_type=j...  30.3 us
    gather x3, other arithmetic, local(): slot_list = block_slot[0][tile_item[0, 0]]  20.1 us
  transfers between devices with their start and end apart: 5, of which 4 were waited for; matrix products, arithmetic and copies ran while one was open for 50% of the time, Pallas kernels for 0%

commit v1 on v0

--- a/solution.py
+++ b/solution.py
@@ -103,7 +103,9 @@
         user_wide, item_gram, precision=lax.Precision.HIGHEST
     )
     item_total = lax.psum_scatter(item_part, "users", scatter_dimension=0, tiled=True)
-    user_gram = lax.psum(gramian(user_factors).astype(jnp.bfloat16), "users").astype(jnp.float32)
+    user_gram = jnp.sum(
+        lax.all_gather(gramian(user_factors).astype(jnp.bfloat16), "users"), axis=0
+    ).astype(jnp.float32)
     item_grad = item_total + grad_scale * gram_weight * jnp.dot(
         own_wide, user_gram, precision=lax.Precision.HIGHEST
     )

time: 559 us -> 446 us (0.80)
  waiting for transfers between devices: 242 us -> 126 us
    psum x1 -> x0, waiting for transfers between devices: 98.7 us -> none  [local(): lax.psum(gramian(user_factors).astype(jnp.bfloat16), 'users')]
    reduce_scatter x1, waiting for transfers between devices: 85.6 us -> 68.4 us  [local(): lax.psum_scatter(item_part, 'users', scatter_dimension=0, tiled=True)]
  transfers between devices with their start and end apart: 5 -> 5, of which waited for: 4 -> 3; matrix products, arithmetic and copies ran while one was open for 50% -> 63% of each run, Pallas kernels for 0% -> 0%
where the time goes in v1:
time: 446 us; the launch traced here: 444 us
  matrix products  213 us (48%)
  waiting for transfers between devices  126 us (28%)
  local copies, waits for them, and re-layouts  53.3 us (12%)
  other arithmetic  36.5 us (8%)
  between operations  15.3 us (3%)
    reduce_scatter x1, waiting for transfers between devices, local(): lax.psum_scatter(item_part, 'users', scatter_dimension=0, tiled=True)  68.4 us
    dot_general x8, matrix products, visit_block(): jnp.einsum('tu,tak->uak', user_hot.astype(jnp.float32), user_terms, preci...  64 us
    dot_general x8, matrix products, visit_block(): jnp.einsum('tp,tak->pak', panel_hot.astype(jnp.float32), item_terms, prec...  41.6 us
    dot_general x8, matrix products, visit_block(): jnp.einsum('tab,tbk->tak', weighted, item_tiles, preferred_element_type=j...  38.1 us
    psum x1, waiting for transfers between devices, local(): user_total = lax.psum(user_part, 'items')  36.4 us
    dot_general x8, matrix products, visit_block(): jnp.einsum('tab,tak->tbk', weighted, user_tiles, preferred_element_type=j...  30.3 us
    gather x3, other arithmetic, local(): slot_list = block_slot[0][tile_item[0, 0]]  20.1 us
    all_gather x1, waiting for transfers between devices, local(): gathered = lax.all_gather(item_factors, 'users', axis=1, tiled=True)[0]  20.1 us
  transfers between devices with their start and end apart: 5, of which 3 were waited for; matrix products, arithmetic and copies ran while one was open for 63% of the time, Pallas kernels for 0%

profile of v1, /device:TPU:0, one launch (start us, length us, event | category | flops | bytes accessed | tf_op | source)
XLA Modules:
  0.0 444.4 jit_solution(16463225676862702576)
XLA Ops:
  21.6 15.7 %select_select_fusion = s32[256]{0:T(256)S(1)} fusion(pred[256]{0:T(512)(128)(4,1)S(1)} %get-tuple-element.366, pred[256]{0:T(512)(128)(4,1)S(1)} %get-tuple-element.365, pred[256]{0:T(512)(128)(4,1)S(1)} %get-tuple-element.364, pred[256]{0:T(512)(128)(4,1)S(1)} %get-tuple-element.363, pred[256]{0:T(512)(128)(4,1)S(1)} %get-tuple-element.362, ...), kind=kLoop, calls=%fused_computation.84 | loop fusion | flops 6400 | bytes 8548 | tf_op jit(solution)/shard_map/gather | solution.py:36
  37.3 20.1 %all-gather.4.cloned.1.call-done = bf16[1,4096,256]{2,1,0:T(8,128)(2,1)} async-done(((bf16[1,128,256]{2,1,0:T(8,128)(2,1)}), bf16[1,4096,256]{2,1,0:T(8,128)(2,1)}) %all-gather.4.cloned.1.call-update) | async-done | bytes 2097168 | tf_op jit(solution)/shard_map/all_gather | solution.py:31
  60.2 232.7 %while.18 = (s32[]{:T(128)}, f32[16,128,256]{2,0,1:T(8,128)}, f32[32,128,256]{2,0,1:T(8,128)}, s32[256]{0:T(256)S(1)}, bf16[256,128,128]{2,1,0:T(8,128)(2,1)}, /...) while((s32[]{:T(128)}, f32[16,128,256]{2,0,1:T(8,128)}, ...), condition=%wide.region_1.0_spmd.clone, body=%wide.region_0.0_spmd.clone.sunk | while | flops 1520438400 | bytes 120588176 | solution.py:94
  70.5 7.4 %select_add_fusion.4 = f32[16,128,256]{2,0,1:T(8,128)} fusion(f32[16,128,256]{2,0,1:T(8,128)} %get-tuple-element.497, f32[32,128,256]{2,1,0:T(8,128)} %fusion.84, pred[]{:T(512)S(6)} %compare.128, s32[32]{0:T(128)S(1)} %dynamic_slice.62), kind=kOutput, calls=%fused_computation.7.clone.1 | convolution fusion | flops 202375680 | bytes 8388737 | tf_op jit(solution)/shard_map/while/body/eval_jaxpr/tu,tak->uak/dot_general | solution.py:79
  81.7 5.2 %select_add_fusion.5 = f32[32,128,256]{2,0,1:T(8,128)S(1)} fusion(f32[32,128,256]{2,0,1:T(8,128)S(1)} %copy-done.2, f32[32,128,256]{2,1,0:T(8,128)S(1)} %fusion.85, pred[]{:T(512)S(6)} %compare.128, s32[32]{0:T(128)S(1)} %dynamic_slice.61), kind=kOutput, calls=%fused_computation.6.clone.1 | convolution fusion | flops 404751360 | bytes 12583041 | tf_op jit(solution)/shard_map/while/body/eval_jaxpr/tp,tak->pak/dot_general | solution.py:82
  99.0 8.1 %select_add_fusion.4 = f32[16,128,256]{2,0,1:T(8,128)} fusion(f32[16,128,256]{2,0,1:T(8,128)} %get-tuple-element.497, f32[32,128,256]{2,1,0:T(8,128)} %fusion.84, pred[]{:T(512)S(6)} %compare.128, s32[32]{0:T(128)S(1)} %dynamic_slice.62), kind=kOutput, calls=%fused_computation.7.clone.1 | convolution fusion | flops 202375680 | bytes 8388737 | tf_op jit(solution)/shard_map/while/body/eval_jaxpr/tu,tak->uak/dot_general | solution.py:79
  110.9 5.2 %select_add_fusion.5 = f32[32,128,256]{2,0,1:T(8,128)S(1)} fusion(f32[32,128,256]{2,0,1:T(8,128)S(1)} %copy-done.2, f32[32,128,256]{2,1,0:T(8,128)S(1)} %fusion.85, pred[]{:T(512)S(6)} %compare.128, s32[32]{0:T(128)S(1)} %dynamic_slice.61), kind=kOutput, calls=%fused_computation.6.clone.1 | convolution fusion | flops 404751360 | bytes 12583041 | tf_op jit(solution)/shard_map/while/body/eval_jaxpr/tp,tak->pak/dot_general | solution.py:82
  128.1 8.1 %select_add_fusion.4 = f32[16,128,256]{2,0,1:T(8,128)} fusion(f32[16,128,256]{2,0,1:T(8,128)} %get-tuple-element.497, f32[32,128,256]{2,1,0:T(8,128)} %fusion.84, pred[]{:T(512)S(6)} %compare.128, s32[32]{0:T(128)S(1)} %dynamic_slice.62), kind=kOutput, calls=%fused_computation.7.clone.1 | convolution fusion | flops 202375680 | bytes 8388737 | tf_op jit(solution)/shard_map/while/body/eval_jaxpr/tu,tak->uak/dot_general | solution.py:79
  140.0 5.2 %select_add_fusion.5 = f32[32,128,256]{2,0,1:T(8,128)S(1)} fusion(f32[32,128,256]{2,0,1:T(8,128)S(1)} %copy-done.2, f32[32,128,256]{2,1,0:T(8,128)S(1)} %fusion.85, pred[]{:T(512)S(6)} %compare.128, s32[32]{0:T(128)S(1)} %dynamic_slice.61), kind=kOutput, calls=%fused_computation.6.clone.1 | convolution fusion | flops 404751360 | bytes 12583041 | tf_op jit(solution)/shard_map/while/body/eval_jaxpr/tp,tak->pak/dot_general | solution.py:82
  157.3 8.1 %select_add_fusion.4 = f32[16,128,256]{2,0,1:T(8,128)} fusion(f32[16,128,256]{2,0,1:T(8,128)} %get-tuple-element.497, f32[32,128,256]{2,1,0:T(8,128)} %fusion.84, pred[]{:T(512)S(6)} %compare.128, s32[32]{0:T(128)S(1)} %dynamic_slice.62), kind=kOutput, calls=%fused_computation.7.clone.1 | convolution fusion | flops 202375680 | bytes 8388737 | tf_op jit(solution)/shard_map/while/body/eval_jaxpr/tu,tak->uak/dot_general | solution.py:79
  169.2 5.2 %select_add_fusion.5 = f32[32,128,256]{2,0,1:T(8,128)S(1)} fusion(f32[32,128,256]{2,0,1:T(8,128)S(1)} %copy-done.2, f32[32,128,256]{2,1,0:T(8,128)S(1)} %fusion.85, pred[]{:T(512)S(6)} %compare.128, s32[32]{0:T(128)S(1)} %dynamic_slice.61), kind=kOutput, calls=%fused_computation.6.clone.1 | convolution fusion | flops 404751360 | bytes 12583041 | tf_op jit(solution)/shard_map/while/body/eval_jaxpr/tp,tak->pak/dot_general | solution.py:82
  186.4 8.1 %select_add_fusion.4 = f32[16,128,256]{2,0,1:T(8,128)} fusion(f32[16,128,256]{2,0,1:T(8,128)} %get-tuple-element.497, f32[32,128,256]{2,1,0:T(8,128)} %fusion.84, pred[]{:T(512)S(6)} %compare.128, s32[32]{0:T(128)S(1)} %dynamic_slice.62), kind=kOutput, calls=%fused_computation.7.clone.1 | convolution fusion | flops 202375680 | bytes 8388737 | tf_op jit(solution)/shard_map/while/body/eval_jaxpr/tu,tak->uak/dot_general | solution.py:79
  198.3 5.2 %select_add_fusion.5 = f32[32,128,256]{2,0,1:T(8,128)S(1)} fusion(f32[32,128,256]{2,0,1:T(8,128)S(1)} %copy-done.2, f32[32,128,256]{2,1,0:T(8,128)S(1)} %fusion.85, pred[]{:T(512)S(6)} %compare.128, s32[32]{0:T(128)S(1)} %dynamic_slice.61), kind=kOutput, calls=%fused_computation.6.clone.1 | convolution fusion | flops 404751360 | bytes 12583041 | tf_op jit(solution)/shard_map/while/body/eval_jaxpr/tp,tak->pak/dot_general | solution.py:82
  215.6 8.1 %select_add_fusion.4 = f32[16,128,256]{2,0,1:T(8,128)} fusion(f32[16,128,256]{2,0,1:T(8,128)} %get-tuple-element.497, f32[32,128,256]{2,1,0:T(8,128)} %fusion.84, pred[]{:T(512)S(6)} %compare.128, s32[32]{0:T(128)S(1)} %dynamic_slice.62), kind=kOutput, calls=%fused_computation.7.clone.1 | convolution fusion | flops 202375680 | bytes 8388737 | tf_op jit(solution)/shard_map/while/body/eval_jaxpr/tu,tak->uak/dot_general | solution.py:79
  227.5 5.2 %select_add_fusion.5 = f32[32,128,256]{2,0,1:T(8,128)S(1)} fusion(f32[32,128,256]{2,0,1:T(8,128)S(1)} %copy-done.2, f32[32,128,256]{2,1,0:T(8,128)S(1)} %fusion.85, pred[]{:T(512)S(6)} %compare.128, s32[32]{0:T(128)S(1)} %dynamic_slice.61), kind=kOutput, calls=%fused_computation.6.clone.1 | convolution fusion | flops 404751360 | bytes 12583041 | tf_op jit(solution)/shard_map/while/body/eval_jaxpr/tp,tak->pak/dot_general | solution.py:82
  244.7 8.1 %select_add_fusion.4 = f32[16,128,256]{2,0,1:T(8,128)} fusion(f32[16,128,256]{2,0,1:T(8,128)} %get-tuple-element.497, f32[32,128,256]{2,1,0:T(8,128)} %fusion.84, pred[]{:T(512)S(6)} %compare.128, s32[32]{0:T(128)S(1)} %dynamic_slice.62), kind=kOutput, calls=%fused_computation.7.clone.1 | convolution fusion | flops 202375680 | bytes 8388737 | tf_op jit(solution)/shard_map/while/body/eval_jaxpr/tu,tak->uak/dot_general | solution.py:79
  256.6 5.2 %select_add_fusion.5 = f32[32,128,256]{2,0,1:T(8,128)S(1)} fusion(f32[32,128,256]{2,0,1:T(8,128)S(1)} %copy-done.2, f32[32,128,256]{2,1,0:T(8,128)S(1)} %fusion.85, pred[]{:T(512)S(6)} %compare.128, s32[32]{0:T(128)S(1)} %dynamic_slice.61), kind=kOutput, calls=%fused_computation.6.clone.1 | convolution fusion | flops 404751360 | bytes 12583041 | tf_op jit(solution)/shard_map/while/body/eval_jaxpr/tp,tak->pak/dot_general | solution.py:82
  273.9 8.1 %select_add_fusion.4 = f32[16,128,256]{2,0,1:T(8,128)} fusion(f32[16,128,256]{2,0,1:T(8,128)} %get-tuple-element.497, f32[32,128,256]{2,1,0:T(8,128)} %fusion.84, pred[]{:T(512)S(6)} %compare.128, s32[32]{0:T(128)S(1)} %dynamic_slice.62), kind=kOutput, calls=%fused_computation.7.clone.1 | convolution fusion | flops 202375680 | bytes 8388737 | tf_op jit(solution)/shard_map/while/body/eval_jaxpr/tu,tak->uak/dot_general | solution.py:79
  285.8 5.2 %select_add_fusion.5 = f32[32,128,256]{2,0,1:T(8,128)S(1)} fusion(f32[32,128,256]{2,0,1:T(8,128)S(1)} %copy-done.2, f32[32,128,256]{2,1,0:T(8,128)S(1)} %fusion.85, pred[]{:T(512)S(6)} %compare.128, s32[32]{0:T(128)S(1)} %dynamic_slice.61), kind=kOutput, calls=%fused_computation.6.clone.1 | convolution fusion | flops 404751360 | bytes 12583041 | tf_op jit(solution)/shard_map/while/body/eval_jaxpr/tp,tak->pak/dot_general | solution.py:82
  303.2 5.1 %broadcast_multiply_fusion = f32[32,128,256]{2,0,1:T(8,128)} fusion(f32[32,128,256]{2,0,1:T(8,128)} %get-tuple-element.290), kind=kLoop, calls=%fused_computation.42 | loop fusion | flops 1048576 | bytes 8388608 | tf_op jit(solution)/shard_map/mul | solution.py:96
  308.3 5.9 %copy.23 = f32[32,128,256]{1,0,2:T(8,128)} copy(f32[32,128,256]{2,0,1:T(8,128)} %broadcast_multiply_fusion) | data formatting | bytes 8388608 | tf_op jit(solution)/shard_map/mul | solution.py:96
  314.2 7.9 %copy.50 = f32[32,8,32,128]{3,1,2,0:T(8,128)} copy(f32[32,8,32,128]{3,2,1,0:T(8,128)} %bitcast.101) | data formatting | bytes 8388608
  322.2 36.4 %all-reduce.3.cloned.1.call-done = f32[2048,256]{0,1:T(8,128)} async-done(((f32[2048,256]{0,1:T(8,128)}), f32[2048,256]{0,1:T(8,128)}) %all-reduce.3.cloned.1.call-update) | async-done | bytes 2097168 | tf_op jit(solution)/shard_map/psum | solution.py:101
  367.0 68.4 %reduce-scatter.2.cloned.1.call-done = f32[128,256]{0,1:T(8,128)} async-done(((f32[4096,256]{0,1:T(8,128)}), f32[128,256]{0,1:T(8,128)}) %reduce-scatter.2.cloned.1.call-update) | async-done | bytes 131088 | tf_op jit(solution)/shard_map/reduce_scatter | solution.py:105
  (199 shorter events, 163.1 us)
Async XLA Ops:
  8.0 9.1 %copy-start.8 = (s32[1,1,256]{2,1,0:T(1,128)S(1)}, s32[1,1,256]{2,1,0:T(1,128)}, u32[]{:S(2)}) copy-start(s32[1,1,256]{2,1,0:T(1,128)} %param.15) | copy-start | bytes 3076
  8.0 49.4 %all-gather.4.cloned.1.call-start = ((), (), s32[]{:S(2)}) async-start(), calls=%async_computation.1 | async-start | bytes 2162688 | tf_op jit(solution)/shard_map/all_gather | solution.py:31
  8.7 313.5 %all-reduce.5.cloned.1.call-start = ((), (), s32[]{:S(2)}) async-start(), calls=%async_computation.3 | async-start | bytes 524288 | tf_op jit(solution)/shard_map/psum | solution.py:100
  10.6 348.0 %all-reduce.3.cloned.1.call-start = ((), (), s32[]{:S(2)}) async-start(), calls=%async_computation.2 | async-start | bytes 4194304 | tf_op jit(solution)/shard_map/psum | solution.py:101
  70.5 7.4 %copy-start.1 = (bf16[32,128,256]{2,0,1:T(8,128)(2,1)S(1)}, bf16[32,128,256]{2,0,1:T(8,128)(2,1)}, u32[]{:S(2)}) copy-start(bf16[32,128,256]{2,0,1:T(8,128)(2,1)} %copy-done) | copy-start | bytes 6291460 | tf_op jit(solution)/shard_map/while
  81.7 7.1 %copy-start.5 = (bf16[32,128,256]{2,0,1:T(8,128)(2,1)S(1)}, bf16[32,128,256]{2,0,1:T(8,128)(2,1)}, u32[]{:S(2)}) copy-start(bf16[32,128,256]{2,0,1:T(8,128)(2,1)} %copy-done.4) | copy-start | bytes 6291460 | tf_op jit(solution)/shard_map/while
  99.0 8.1 %copy-start.1 = (bf16[32,128,256]{2,0,1:T(8,128)(2,1)S(1)}, bf16[32,128,256]{2,0,1:T(8,128)(2,1)}, u32[]{:S(2)}) copy-start(bf16[32,128,256]{2,0,1:T(8,128)(2,1)} %copy-done) | copy-start | bytes 6291460 | tf_op jit(solution)/shard_map/while
  110.9 7.1 %copy-start.5 = (bf16[32,128,256]{2,0,1:T(8,128)(2,1)S(1)}, bf16[32,128,256]{2,0,1:T(8,128)(2,1)}, u32[]{:S(2)}) copy-start(bf16[32,128,256]{2,0,1:T(8,128)(2,1)} %copy-done.4) | copy-start | bytes 6291460 | tf_op jit(solution)/shard_map/while
  128.1 8.1 %copy-start.1 = (bf16[32,128,256]{2,0,1:T(8,128)(2,1)S(1)}, bf16[32,128,256]{2,0,1:T(8,128)(2,1)}, u32[]{:S(2)}) copy-start(bf16[32,128,256]{2,0,1:T(8,128)(2,1)} %copy-done) | copy-start | bytes 6291460 | tf_op jit(solution)/shard_map/while
  136.2 3.8 copy-start.2
  140.0 7.2 %copy-start.5 = (bf16[32,128,256]{2,0,1:T(8,128)(2,1)S(1)}, bf16[32,128,256]{2,0,1:T(8,128)(2,1)}, u32[]{:S(2)}) copy-start(bf16[32,128,256]{2,0,1:T(8,128)(2,1)} %copy-done.4) | copy-start | bytes 6291460 | tf_op jit(solution)/shard_map/while
  157.3 8.1 %copy-start.1 = (bf16[32,128,256]{2,0,1:T(8,128)(2,1)S(1)}, bf16[32,128,256]{2,0,1:T(8,128)(2,1)}, u32[]{:S(2)}) copy-start(bf16[32,128,256]{2,0,1:T(8,128)(2,1)} %copy-done) | copy-start | bytes 6291460 | tf_op jit(solution)/shard_map/while
  169.2 7.1 %copy-start.5 = (bf16[32,128,256]{2,0,1:T(8,128)(2,1)S(1)}, bf16[32,128,256]{2,0,1:T(8,128)(2,1)}, u32[]{:S(2)}) copy-start(bf16[32,128,256]{2,0,1:T(8,128)(2,1)} %copy-done.4) | copy-start | bytes 6291460 | tf_op jit(solution)/shard_map/while
  186.4 8.1 %copy-start.1 = (bf16[32,128,256]{2,0,1:T(8,128)(2,1)S(1)}, bf16[32,128,256]{2,0,1:T(8,128)(2,1)}, u32[]{:S(2)}) copy-start(bf16[32,128,256]{2,0,1:T(8,128)(2,1)} %copy-done) | copy-start | bytes 6291460 | tf_op jit(solution)/shard_map/while
  198.3 7.2 %copy-start.5 = (bf16[32,128,256]{2,0,1:T(8,128)(2,1)S(1)}, bf16[32,128,256]{2,0,1:T(8,128)(2,1)}, u32[]{:S(2)}) copy-start(bf16[32,128,256]{2,0,1:T(8,128)(2,1)} %copy-done.4) | copy-start | bytes 6291460 | tf_op jit(solution)/shard_map/while
  215.6 8.1 %copy-start.1 = (bf16[32,128,256]{2,0,1:T(8,128)(2,1)S(1)}, bf16[32,128,256]{2,0,1:T(8,128)(2,1)}, u32[]{:S(2)}) copy-start(bf16[32,128,256]{2,0,1:T(8,128)(2,1)} %copy-done) | copy-start | bytes 6291460 | tf_op jit(solution)/shard_map/while
  227.5 7.1 %copy-start.5 = (bf16[32,128,256]{2,0,1:T(8,128)(2,1)S(1)}, bf16[32,128,256]{2,0,1:T(8,128)(2,1)}, u32[]{:S(2)}) copy-start(bf16[32,128,256]{2,0,1:T(8,128)(2,1)} %copy-done.4) | copy-start | bytes 6291460 | tf_op jit(solution)/shard_map/while
  244.7 8.1 %copy-start.1 = (bf16[32,128,256]{2,0,1:T(8,128)(2,1)S(1)}, bf16[32,128,256]{2,0,1:T(8,128)(2,1)}, u32[]{:S(2)}) copy-start(bf16[32,128,256]{2,0,1:T(8,128)(2,1)} %copy-done) | copy-start | bytes 6291460 | tf_op jit(solution)/shard_map/while
  256.6 7.2 %copy-start.5 = (bf16[32,128,256]{2,0,1:T(8,128)(2,1)S(1)}, bf16[32,128,256]{2,0,1:T(8,128)(2,1)}, u32[]{:S(2)}) copy-start(bf16[32,128,256]{2,0,1:T(8,128)(2,1)} %copy-done.4) | copy-start | bytes 6291460 | tf_op jit(solution)/shard_map/while
  273.9 8.1 %copy-start.1 = (bf16[32,128,256]{2,0,1:T(8,128)(2,1)S(1)}, bf16[32,128,256]{2,0,1:T(8,128)(2,1)}, u32[]{:S(2)}) copy-start(bf16[32,128,256]{2,0,1:T(8,128)(2,1)} %copy-done) | copy-start | bytes 6291460 | tf_op jit(solution)/shard_map/while
  285.8 7.1 %copy-start.5 = (bf16[32,128,256]{2,0,1:T(8,128)(2,1)S(1)}, bf16[32,128,256]{2,0,1:T(8,128)(2,1)}, u32[]{:S(2)}) copy-start(bf16[32,128,256]{2,0,1:T(8,128)(2,1)} %copy-done.4) | copy-start | bytes 6291460 | tf_op jit(solution)/shard_map/while
  300.8 63.2 %all-gather.6.cloned.1.call-start = ((), (), s32[]{:S(2)}) async-start(), calls=%async_computation.5 | async-start | bytes 4325376 | tf_op jit(solution)/shard_map/all_gather | solution.py:107
  303.2 132.2 %reduce-scatter.2.cloned.1.call-start = ((), (), s32[]{:S(2)}) async-start(), calls=%async_computation.4 | async-start | bytes 4325376 | tf_op jit(solution)/shard_map/reduce_scatter | solution.py:105
  364.0 71.3 %copy-start.7 = (bf16[1,128,256]{2,1,0:T(8,128)(2,1)S(1)}, bf16[1,128,256]{2,1,0:T(8,128)(2,1)}, u32[]{:S(2)}) copy-start(bf16[1,128,256]{2,1,0:T(8,128)(2,1)} %param.11) | copy-start | bytes 196612
  (33 other events, 76.2 us)
Sparse Core Ops, SparseCore 0:
  11.1 46.2 all-gather.3
  304.5 45.3 all-gather.5
  353.5 81.7 reduce-scatter.1
Sparse Core Ops, SparseCore 1:
  14.0 147.1 all-reduce.4
  300.9 57.7 all-reduce.2
